TPU v7x, 32 devices: a whole 2x2x4 slice. The times are simulated.
32 devices in a mesh: dp: 4 (over y, x), ctx: 4 (over z), tensor: 2 (over core).
Axes of the slice: x: 2, y: 2, z: 4, core: 2. Of those that a mesh axis runs over, the one named last changes fastest.
Arguments:
- hidden: bfloat16 [4, 1024, 1024], P('dp', 'ctx'), may hold values from -6 to 6
- segment_ids: int32 [4, 1024], P('dp', 'ctx'), may hold values from 0 to 5, as said below
- cotangent: bfloat16 [4, 1024, 1024], P('dp', 'ctx'), may hold values from -6 to 6
- input_gain: float32 [1024], replicated, may hold values from 0.5 to 1.5
- gate_weight: bfloat16 [1024, 2048], P('dp', 'tensor'), may hold values from -0.1875 to 0.1875
- value_weight: bfloat16 [1024, 2048], P('dp', 'tensor'), may hold values from -0.1875 to 0.1875
- state_weight: bfloat16 [1024, 256], P('dp'), may hold values from -0.1875 to 0.1875
- step_weight: bfloat16 [1024, 32], P('dp', 'tensor'), may hold values from -0.1875 to 0.1875
- conv_weight: float32 [4, 2304], replicated, may hold values from -3 to 3
- conv_bias: float32 [2304], replicated, may hold values from -3 to 3
- step_bias: float32 [32], replicated, may hold values from -4 to -1
- decay_log: float32 [32], replicated, may hold values from -6.5 to -1.5
- skip_gain: float32 [32], replicated, may hold values from 0.5 to 1.5
- mixer_gain: float32 [2048], replicated, may hold values from 0.5 to 1.5
- out_weight: bfloat16 [2048, 1024], P('tensor', 'dp'), may hold values from -0.125 to 0.125
Outputs:
- output: bfloat16 [4, 1024, 1024], P('dp', 'ctx')
- grad_hidden: float32 [4, 1024, 1024], P('dp', 'ctx')
- grad_input_gain: float32 [1024], replicated
- grad_gate_weight: float32 [1024, 2048], P('dp', 'tensor')
- grad_value_weight: float32 [1024, 2048], P('dp', 'tensor')
- grad_state_weight: float32 [1024, 256], P('dp')
- grad_step_weight: float32 [1024, 32], P('dp', 'tensor')
- grad_conv_weight: float32 [4, 2304], replicated
- grad_conv_bias: float32 [2304], replicated
- grad_step_bias: float32 [32], replicated
- grad_decay_log: float32 [32], replicated
- grad_skip_gain: float32 [32], replicated
- grad_mixer_gain: float32 [2048], replicated
- grad_out_weight: float32 [2048, 1024], P('tensor', 'dp')
Inputs may be any that keep to these rules, and one draw needn't show every extreme that they name: `segment_ids`: within each sequence the ids start at 0, never fall and rise by one at each new document. Every document has 200 to 512 tokens, except the last one of a sequence, which may be cut short by the sequence's end. The first document of the first sequence has exactly 512 tokens; every document of the last sequence has exactly 200 tokens (the final one possibly cut short).
All inputs are finite; a program needn't handle non-finite values.
Results may differ from a plain program's by a relative error of at most 0.014.
Values may be sent and summed in bfloat16 or wider, within the bound.
A program may use at most 192 MiB of HBM per device.

v0:
```python
from functools import partial
import jax
import jax.numpy as jnp
from jax import lax
from jax.sharding import PartitionSpec as P

GROUP = 128
epsilon = 1e-05
highest = lax.Precision.HIGHEST


def shifted(array, axis, by):
    size = lax.axis_size(axis)
    pairs = [(i, i + by) for i in range(size) if 0 <= i + by < size]
    return lax.ppermute(array, axis, pairs)


def carried_in_2(array, axis, combine, identity):
    size, here = (lax.axis_size(axis), lax.axis_index(axis))
    everything = jax.tree.map(
        lambda part, kind: lax.all_gather(part.astype(kind), axis),
        array,
        (jnp.bfloat16, jnp.bfloat16),
    )
    start = jax.tree.map(
        lambda part, zero: jnp.broadcast_to(jnp.asarray(zero, part.dtype), part.shape),
        array,
        identity,
    )

    def turn(k, before):
        reached = k < here
        new = combine(
            before, jax.tree.map(lambda part, own: part[k].astype(own.dtype), everything, array)
        )
        return jax.tree.map(lambda a, b: jnp.where(reached, a, b), new, before)

    return lax.fori_loop(0, size, turn, start)


def prefix(array, axis, join, neutral):
    count = lax.axis_size(axis)
    place = lax.axis_index(axis)
    ahead = count - 1 - place
    gathered = jax.tree.map(
        lambda a, kind: lax.all_gather(a.astype(kind), axis),
        array,
        jax.tree.map(lambda a: jnp.bfloat16 if a.dtype == jnp.float32 else a.dtype, array),
    )
    state = jax.tree.map(lambda a, e: jnp.zeros_like(a) + jnp.asarray(e, a.dtype), array, neutral)

    def one(turn, state):
        source = count - 1 - turn
        return join(
            state,
            jax.tree.map(
                lambda a, own: lax.dynamic_index_in_dim(a, source, 0, False).astype(own.dtype),
                gathered,
                array,
            ),
        )

    return lax.fori_loop(0, ahead, one, state)


def rms_scale(values, scaling):
    return values * lax.rsqrt(jnp.mean(values * values, axis=-1, keepdims=True) + epsilon) * scaling


def group_step(carry, item, rates):
    values, inputs_b, inputs_c, delta, segments, previous = item
    log_decay = delta * rates[None, :]
    running = jnp.cumsum(log_decay, axis=0)
    length = segments.shape[0]
    order = jnp.arange(length)
    allowed = (segments[:, None] == segments[None, :]) & (order[:, None] >= order[None, :])
    spread = running.T[:, :, None] - running.T[:, None, :]
    decay = jnp.where(allowed[None], jnp.exp(jnp.where(allowed[None], spread, 0.0)), 0.0)
    scores = jnp.dot(inputs_c, inputs_b.T, precision=highest)
    mixing = decay * scores[None] * delta.T[:, None, :]
    inner = jnp.einsum("hts,shp->thp", mixing, values, precision=highest)
    entry = jnp.exp(running) * (segments == previous).astype(jnp.float32)[:, None]
    carried = jnp.einsum("tn,hpn->thp", inputs_c, carry, precision=highest) * entry[:, :, None]
    tail = (
        jnp.exp(running[-1][None, :] - running)
        * (segments == segments[-1]).astype(jnp.float32)[:, None]
        * delta
    )
    fade = jnp.exp(running[-1]) * (segments[-1] == previous).astype(jnp.float32)
    update = jnp.einsum("sh,shp,sn->hpn", tail, values, inputs_b, precision=highest)
    return (carry * fade[:, None, None] + update, inner + carried)


def combine_states(earlier, later):
    return (earlier[0] * later[0], later[0][:, None, None] * earlier[1] + later[1])


def body(
    hidden,
    segment_ids,
    cotangent,
    input_gain,
    gate_weight,
    value_weight,
    state_weight,
    step_weight,
    conv_weight,
    conv_bias,
    step_bias,
    decay_log,
    skip_gain,
    mixer_gain,
    out_weight,
):
    tokens = hidden[0]
    wrapped = segment_ids[0] % 128
    cotangent_rows = cotangent[0]
    length = tokens.shape[0]
    width = tokens.shape[1]
    shard = lax.axis_index("tensor")
    shards = lax.axis_size("tensor")
    full_gate, full_value, full_state, full_step, full_out = (
        lax.all_gather(gate_weight, "dp", axis=0, tiled=True),
        lax.all_gather(value_weight, "dp", axis=0, tiled=True),
        lax.all_gather(state_weight, "dp", axis=0, tiled=True),
        lax.all_gather(step_weight, "dp", axis=0, tiled=True),
        lax.all_gather(out_weight, "dp", axis=1, tiled=True),
    )
    local_width = full_gate.shape[1]
    local_heads = full_step.shape[1]
    head_size = local_width // local_heads
    inner_width = local_width * shards
    states = full_state.shape[1] // 2
    reach = conv_weight.shape[0] - 1
    base = tokens.astype(jnp.float32)
    normed_full, norm_back = jax.vjp(rms_scale, base, input_gain)
    normed = normed_full.astype(jnp.bfloat16)
    gate = jnp.dot(normed, full_gate, preferred_element_type=jnp.float32)
    value_pre = jnp.dot(normed, full_value, preferred_element_type=jnp.float32).astype(jnp.bfloat16)
    state_pre = jnp.dot(normed, full_state, preferred_element_type=jnp.float32).astype(jnp.bfloat16)
    raw_step = jnp.dot(normed, full_step, preferred_element_type=jnp.float32)
    conv_input = jnp.concatenate([value_pre, state_pre], 1)
    edge_rows, edge_ids = shifted(
        (conv_input[length - reach :], wrapped[length - reach :].astype(jnp.bfloat16)), "ctx", 1
    )
    padded = jnp.concatenate([edge_rows, conv_input], 0).astype(jnp.float32)
    padded_ids = jnp.concatenate([edge_ids.astype(jnp.int32), wrapped])
    before = padded_ids[reach - 1]
    kernel = jnp.concatenate(
        [
            lax.dynamic_slice_in_dim(conv_weight, shard * local_width, local_width, 1),
            conv_weight[:, inner_width:],
        ],
        1,
    )
    offset = jnp.concatenate(
        [
            lax.dynamic_slice_in_dim(conv_bias, shard * local_width, local_width, 0),
            conv_bias[inner_width:],
        ],
        0,
    )
    local_bias = lax.dynamic_slice_in_dim(step_bias, shard * local_heads, local_heads, 0)
    local_decay = lax.dynamic_slice_in_dim(decay_log, shard * local_heads, local_heads, 0)
    local_skip = lax.dynamic_slice_in_dim(skip_gain, shard * local_heads, local_heads, 0)
    local_gain = lax.dynamic_slice_in_dim(mixer_gain, shard * local_width, local_width, 0)

    def activate(padded_rows, raw_rows, taps, shift_bias, bias_heads):
        total = jnp.broadcast_to(shift_bias[None, :], (length, shift_bias.shape[0]))
        for lag in range(reach + 1):
            begin = reach - lag
            same = (padded_ids[begin : begin + length] == wrapped).astype(jnp.float32)
            total = total + taps[lag][None, :] * padded_rows[begin : begin + length] * same[:, None]
        activated = jax.nn.silu(total)
        values = activated[:, :local_width].reshape(length, local_heads, head_size)
        return (
            values,
            activated[:, local_width : local_width + states],
            activated[:, local_width + states :],
            jax.nn.softplus(raw_rows + bias_heads[None, :]),
        )

    (values, inputs_b, inputs_c, delta), activate_back = jax.vjp(
        activate, padded, raw_step, kernel, offset, local_bias
    )

    def block(values_in, map_in, map_out, delta_in, decay_in, skip_in):
        rates = -jnp.exp(decay_in)
        count = length // GROUP
        previous = jnp.concatenate([before[None], wrapped[GROUP - 1 :: GROUP][: count - 1]])
        items = (
            values_in.reshape(count, GROUP, local_heads, head_size),
            map_in.reshape(count, GROUP, states),
            map_out.reshape(count, GROUP, states),
            delta_in.reshape(count, GROUP, local_heads),
            wrapped.reshape(count, GROUP),
            previous,
        )
        final, outputs = lax.scan(
            partial(group_step, rates=rates),
            jnp.zeros((local_heads, head_size, states), jnp.float32),
            items,
        )
        mixed = outputs.reshape(length, local_heads, head_size) + skip_in[None, :, None] * values_in
        through = jnp.exp(jnp.sum(delta_in * rates[None, :], axis=0)) * (
            wrapped[-1] == before
        ).astype(jnp.float32)
        return (mixed, through, final)

    (mixed_own, through, final), block_back = jax.vjp(
        block, values, inputs_b, inputs_c, delta, local_decay, local_skip
    )
    carried_in = carried_in_2(
        (through, final), "ctx", combine_states, (jnp.ones_like(through), jnp.zeros_like(final))
    )
    entering = carried_in[1]

    def enter(map_out, delta_in, decay_in, state_in):
        running = jnp.cumsum(delta_in * (-jnp.exp(decay_in))[None, :], axis=0)
        scaling = jnp.exp(running) * (wrapped == before).astype(jnp.float32)[:, None]
        return jnp.einsum("tn,hpn->thp", map_out, state_in, precision=highest) * scaling[:, :, None]

    added, enter_back = jax.vjp(enter, inputs_c, delta, local_decay, entering)
    mixed = (mixed_own + added).reshape(length, local_width)
    silu_gate = jax.nn.silu(gate)
    product = mixed * silu_gate
    squares = lax.psum(jnp.sum(product * product, axis=1), "tensor")
    scale = lax.rsqrt(squares / inner_width + epsilon)
    unit = product * scale[:, None]
    gated = (unit * local_gain[None, :]).astype(jnp.bfloat16)
    branch_out = jnp.dot(gated, full_out, preferred_element_type=jnp.float32)
    summed = lax.psum(branch_out.astype(jnp.bfloat16), "tensor").astype(jnp.float32)
    result = (base + summed).astype(jnp.bfloat16)
    grad_gated = jnp.dot(cotangent_rows, full_out.T, preferred_element_type=jnp.float32)
    grad_out = jnp.dot(gated.T, cotangent_rows, preferred_element_type=jnp.float32)
    grad_mgain = jnp.sum(grad_gated * unit, axis=0)
    grad_unit = grad_gated * local_gain[None, :]
    project = lax.psum(jnp.sum(grad_unit * unit, axis=1), "tensor")
    grad_product = scale[:, None] * (grad_unit - unit * (project / inner_width)[:, None])
    grad_mixed = (grad_product * silu_gate).reshape(length, local_heads, head_size)
    sigma = jax.nn.sigmoid(gate)
    grad_gate = grad_product * mixed * sigma * (1.0 + gate * (1.0 - sigma))
    map_one, delta_one, decay_one, grad_entering = enter_back(grad_mixed)
    carried_out = prefix(
        (through, grad_entering),
        "ctx",
        combine_states,
        (jnp.ones_like(through), jnp.zeros_like(grad_entering)),
    )
    grad_final = carried_out[1]
    grad_through = jnp.sum(grad_final * entering, axis=(1, 2))
    grad_values, grad_map_in, map_two, delta_two, decay_two, grad_skip = block_back(
        (grad_mixed, grad_through, grad_final)
    )
    grad_padded, grad_raw, grad_kernel, grad_offset, grad_bias = activate_back(
        (grad_values, grad_map_in, map_one + map_two, delta_one + delta_two)
    )
    edge_grad = shifted(grad_padded[:reach], "ctx", -1)
    grad_input = grad_padded[reach:].at[length - reach :].add(edge_grad)
    low_gate = grad_gate.astype(jnp.bfloat16)
    low_input = grad_input.astype(jnp.bfloat16)
    low_step = grad_raw.astype(jnp.bfloat16)
    normed_part = (
        jnp.dot(low_gate, full_gate.T, preferred_element_type=jnp.float32)
        + jnp.dot(low_input[:, :local_width], full_value.T, preferred_element_type=jnp.float32)
        + jnp.dot(low_input[:, local_width:], full_state.T, preferred_element_type=jnp.float32)
        + jnp.dot(low_step, full_step.T, preferred_element_type=jnp.float32)
    )
    grad_normed = lax.psum(normed_part.astype(jnp.bfloat16), "tensor").astype(jnp.float32)
    grad_base, grad_gain = norm_back(grad_normed)
    grad_tokens = cotangent_rows.astype(jnp.float32) + grad_base
    grad_gate_w = jnp.dot(normed.T, low_gate, preferred_element_type=jnp.float32)
    grad_value_w = jnp.dot(normed.T, low_input[:, :local_width], preferred_element_type=jnp.float32)
    grad_state_w = jnp.dot(normed.T, low_input[:, local_width:], preferred_element_type=jnp.float32)
    grad_step_w = jnp.dot(normed.T, low_step, preferred_element_type=jnp.float32)
    pieces = (
        lax.psum_scatter(
            grad_gate_w.astype(jnp.bfloat16), "dp", scatter_dimension=0, tiled=True
        ).astype(jnp.float32),
        lax.psum_scatter(
            grad_value_w.astype(jnp.bfloat16), "dp", scatter_dimension=0, tiled=True
        ).astype(jnp.float32),
        lax.psum_scatter(
            grad_step_w.astype(jnp.bfloat16), "dp", scatter_dimension=0, tiled=True
        ).astype(jnp.float32),
        lax.psum_scatter(
            grad_out.astype(jnp.bfloat16), "dp", scatter_dimension=1, tiled=True
        ).astype(jnp.float32),
    )
    sums = (
        lax.psum(pieces[0].astype(jnp.bfloat16), "ctx").astype(jnp.float32),
        lax.psum(pieces[1].astype(jnp.bfloat16), "ctx").astype(jnp.float32),
        lax.psum(pieces[2].astype(jnp.bfloat16), "ctx").astype(jnp.float32),
        lax.psum(pieces[3].astype(jnp.bfloat16), "ctx").astype(jnp.float32),
    )
    halves = width // shards
    keep_half = (jnp.arange(width) // halves == shard).astype(jnp.float32)
    gain_term = grad_gain * keep_half
    kernel_term = jnp.zeros((reach + 1, inner_width + 2 * states), jnp.float32)
    kernel_term = lax.dynamic_update_slice(
        kernel_term, grad_kernel[:, :local_width], (0, shard * local_width)
    )
    kernel_term = kernel_term.at[:, inner_width:].set(grad_kernel[:, local_width:])
    offset_term = jnp.zeros((inner_width + 2 * states,), jnp.float32)
    offset_term = lax.dynamic_update_slice(
        offset_term, grad_offset[:local_width], (shard * local_width,)
    )
    offset_term = offset_term.at[inner_width:].set(grad_offset[local_width:])
    heads_total = local_heads * shards
    bias_term = lax.dynamic_update_slice(
        jnp.zeros((heads_total,), jnp.float32), grad_bias, (shard * local_heads,)
    )
    decay_term = lax.dynamic_update_slice(
        jnp.zeros((heads_total,), jnp.float32), decay_one + decay_two, (shard * local_heads,)
    )
    skip_term = lax.dynamic_update_slice(
        jnp.zeros((heads_total,), jnp.float32), grad_skip, (shard * local_heads,)
    )
    mgain_term = lax.dynamic_update_slice(
        jnp.zeros((inner_width,), jnp.float32), grad_mgain, (shard * local_width,)
    )
    totals = lax.psum(
        (
            gain_term,
            kernel_term,
            offset_term,
            bias_term,
            decay_term,
            skip_term,
            mgain_term,
            grad_state_w,
        ),
        ("dp", "ctx", "tensor"),
    )
    rows = state_weight.shape[0]
    state_rows = lax.dynamic_slice_in_dim(totals[7], lax.axis_index("dp") * rows, rows, 0)
    return (
        result[None],
        grad_tokens[None],
        totals[0],
        sums[0],
        sums[1],
        state_rows,
        sums[2],
        totals[1],
        totals[2],
        totals[3],
        totals[4],
        totals[5],
        totals[6],
        sums[3],
    )


def solution(mesh):
    in_specs = (
        P("dp", "ctx", None),
        P("dp", "ctx"),
        P("dp", "ctx", None),
        P(),
        P("dp", "tensor"),
        P("dp", "tensor"),
        P("dp", None),
        P("dp", "tensor"),
        P(),
        P(),
        P(),
        P(),
        P(),
        P(),
        P("tensor", "dp"),
    )
    out_specs = (
        P("dp", "ctx", None),
        P("dp", "ctx", None),
        P(),
        P("dp", "tensor"),
        P("dp", "tensor"),
        P("dp", None),
        P("dp", "tensor"),
        P(),
        P(),
        P(),
        P(),
        P(),
        P(),
        P("tensor", "dp"),
    )
    return jax.shard_map(body, mesh=mesh, in_specs=in_specs, out_specs=out_specs, check_vma=False)
```

profile of v0, /device:TPU:0, one launch (start us, length us, event | category | flops | bytes accessed | tf_op | source)
XLA Modules:
  0.0 726.9 jit_solution(9285679522740016677)
XLA Ops:
  8.9 4.9 collective-permute-start
  15.5 8.6 %all_gather.33 = bf16[1024,16]{0,1:T(8,128)(2,1)S(1)} all-gather(bf16[256,16]{0,1:T(8,128)(2,1)} %param.36), channel_id=1, replica_groups=mesh['dp'=4,'ctx'=4,'tensor'=2] {'dp'}, dimensions={0}, use_global_device_ids=true | all-gather | bytes 40960 | tf_op jit(solution)/shard_map/all_gather | solution.py:126
  26.1 2.6 compare_select_fusion.3
  29.5 13.2 %all_gather.35 = bf16[1024,256]{1,0:T(8,128)(2,1)S(1)} all-gather(bf16[256,256]{1,0:T(8,128)(2,1)S(1)} %copy-done.49), channel_id=1, replica_groups=mesh['dp'=4,'ctx'=4,'tensor'=2] {'dp'}, dimensions={0}, use_global_device_ids=true | all-gather | bytes 655360 | tf_op jit(solution)/shard_map/all_gather | solution.py:125
  46.3 2.9 all-gather.9.cloned.1.call-done
  49.2 2.3 convolution_convert_fusion.4
  51.6 3.4 collective-permute-start.1
  67.7 120.8 %while.117 = (s32[]{:T(128)}, f32[16,64,128]{2,1,0:T(8,128)S(1)}, f32[2,128,16,64]{1,0,3,2:T(2,128)}, pred[2,16,128,128]{3,2,1,0:T(32,128)(4,1)}, f32[2,16,128,1...) while((s32[]{:T(128)}, f32[16,64,128]{2,1,0:T(8,128)S(1)}, ...), condition=%wide.region_3.4_spmd.clone, body=%wide.region_1.3_spmd.clone.sunk | while | flops 633275392 | bytes 14210707 | solution.py:199
  76.4 3.3 multiply_dynamic-update-slice_fusion.3
  85.8 3.0 fusion.255
  88.8 13.1 %dynamic_update_slice.320 = f32[2,128,16,64]{1,0,3,2:T(2,128)} dynamic-update-slice(f32[2,128,16,64]{1,0,3,2:T(2,128)} %get-tuple-element.2790, f32[1,128,16,64]{1,0,3,2:T(1,128)} %bitcast.578, s32[]{:T(128)} %get-tuple-element.2788, s32[]{:T(128)} %constant.380.clone.1..sunk.1, s32[]{:T(128)} %constant.380.clone.1..sunk.1, s32[]{:T(128)} %constant.380.clone.1..sunk.1) | dynamic-update-slice | bytes 1048580 | tf_op jit(solution)/shard_map/jvp()/while/body/jit(dynamic_update_index_in_dim)/dynamic_update_slice | solution.py:199
  136.7 3.4 multiply_dynamic-update-slice_fusion.3
  146.2 3.0 fusion.255
  149.2 13.1 %dynamic_update_slice.320 = f32[2,128,16,64]{1,0,3,2:T(2,128)} dynamic-update-slice(f32[2,128,16,64]{1,0,3,2:T(2,128)} %get-tuple-element.2790, f32[1,128,16,64]{1,0,3,2:T(1,128)} %bitcast.578, s32[]{:T(128)} %get-tuple-element.2788, s32[]{:T(128)} %constant.380.clone.1..sunk.1, s32[]{:T(128)} %constant.380.clone.1..sunk.1, s32[]{:T(128)} %constant.380.clone.1..sunk.1) | dynamic-update-slice | bytes 1048580 | tf_op jit(solution)/shard_map/jvp()/while/body/jit(dynamic_update_index_in_dim)/dynamic_update_slice | solution.py:199
  195.1 13.5 %all-reduce.13 = bf16[64]{0:T(256)(128)(2,1)S(1)} all-reduce(bf16[64]{0:T(256)(128)(2,1)S(1)} %dynamic-update-slice.8), channel_id=2, replica_groups=mesh['dp'=4,'ctx'=4,'tensor'=2] {'ctx'}, use_global_device_ids=true, to_apply=%add.13 | all-reduce | flops 64 | bytes 256
  208.7 3.0 reshape.727
  211.7 6.7 all-gather.15.cloned.1.call-done
  218.5 4.6 while.118
  223.1 3.8 multiply_add_fusion.2
  226.9 2.6 copy.192
  229.6 25.3 %all-gather.11.cloned.1.call-done = bf16[1024,1024]{1,0:T(8,128)(2,1)} async-done(((bf16[256,1024]{1,0:T(8,128)(2,1)}), bf16[1024,1024]{1,0:T(8,128)(2,1)}) %all-gather.11.cloned.1.call-update) | async-done | bytes 2097168 | tf_op jit(solution)/shard_map/all_gather | solution.py:123
  254.9 3.7 multiply_reduce_fusion.9
  258.6 2.4 psum.112
  261.0 30.6 %all-gather.13.cloned.1.call-done = bf16[1024,1024]{1,0:T(8,128)(2,1)} async-done(((bf16[1024,256]{1,0:T(8,128)(2,1)}), bf16[1024,1024]{1,0:T(8,128)(2,1)}) %all-gather.13.cloned.1.call-update) | async-done | bytes 2097168 | tf_op jit(solution)/shard_map/all_gather | solution.py:127
  291.7 4.0 multiply_reduce_fusion.5
  295.7 2.4 psum.114
  298.1 4.6 multiply_reduce_fusion.6
  304.0 2.9 convolution_convert_fusion.5
  307.0 3.5 convolution_convert_fusion
  313.2 2.5 copy.200
  318.0 17.1 %all-gather.17.cloned.1.call-done = bf16[64,64,128]{2,1,0:T(8,128)(2,1)} async-done(((bf16[16,64,128]{2,1,0:T(8,128)(2,1)}), bf16[64,64,128]{2,1,0:T(8,128)(2,1)}) %all-gather.17.cloned.1.call-update) | async-done | bytes 1048592 | tf_op jit(solution)/shard_map/all_gather | solution.py:46
  335.1 3.7 while.116
  342.0 62.0 %while.119 = (s32[]{:T(128)}, f32[16]{0:T(128)}, f32[16,64,128]{2,1,0:T(8,128)S(1)}, f32[2,128,16,64]{1,3,2,0:T(8,128)}, f32[2,128,128]{2,1,0:T(8,128)}, /*index...) while((s32[]{:T(128)}, f32[16]{0:T(128)}, ...), condition=%wide.region_26.27_spmd.clone, body=%wide.region_16.26_spmd.clone.sunk | while | flops 1263052800 | bytes 29513872 | solution.py:199
  346.4 4.8 fusion.271
  377.2 4.8 fusion.271
  404.0 3.3 copy.219
  407.4 2.4 reshape.775
  418.0 3.8 collective-permute-done.2
  425.9 2.5 reduce-window.16
  428.5 2.6 fusion.195
  435.9 2.5 convolution_add_fusion.6
  441.3 16.5 %reduce-scatter.7.cloned.1.call-done = bf16[256,1024]{1,0:T(8,128)(2,1)} async-done(((bf16[1024,1024]{1,0:T(8,128)(2,1)}), bf16[256,1024]{1,0:T(8,128)(2,1)}) %reduce-scatter.7.cloned.1.call-update) | async-done | bytes 524304 | tf_op jit(solution)/shard_map/reduce_scatter | solution.py:280
  458.6 25.4 %reduce-scatter.9.cloned.1.call-done = bf16[256,16]{0,1:T(8,128)(2,1)} async-done(((bf16[1024,16]{0,1:T(8,128)(2,1)}), bf16[256,16]{0,1:T(8,128)(2,1)}) %reduce-scatter.9.cloned.1.call-update) | async-done | bytes 8208 | tf_op jit(solution)/shard_map/reduce_scatter | solution.py:283
  484.0 11.9 %psum.120 = bf16[256,16]{0,1:T(8,128)(2,1)S(1)} all-reduce(bf16[256,16]{0,1:T(8,128)(2,1)} %reduce-scatter.9.cloned.1.call-done), channel_id=1, replica_groups=mesh['dp'=4,'ctx'=4,'tensor'=2] {'ctx'}, use_global_device_ids=true, to_apply=%region_41.42 | all-reduce | flops 4096 | bytes 16384 | tf_op jit(solution)/shard_map/psum | solution.py:293
  496.5 123.7 %all-reduce.21.cloned.1.call-done = f32[1024,256]{1,0:T(8,128)} async-done(((f32[1024,256]{1,0:T(8,128)}), f32[1024,256]{1,0:T(8,128)}) %all-reduce.21.cloned.1.call-update) | async-done | bytes 1048592 | tf_op jit(solution)/shard_map/psum | solution.py:322
  621.9 19.8 %all-reduce.25.cloned.1.call-done = (bf16[256,1024]{1,0:T(8,128)(2,1)}, bf16[256,1024]{1,0:T(8,128)(2,1)}) async-done(((bf16[256,1024]{1,0:T(8,128)(2,1)}, bf16[256,1024]{1,0:T(8,128)(2,1)}), (bf16[256,1024]{1,0:T(8,128)(2,1)}, bf16[256,1024]{1,0:T(8,128)(2,1)})) %all-reduce.25.cloned.1.call-update) | async-done | bytes 1048592 | tf_op jit(solution)/shard_map/psum | solution.py:232
  643.3 44.3 %all-reduce.14 = (f32[1024]{0:T(1024)}, f32[4,2304]{1,0:T(4,128)}, f32[2304]{0:T(1024)}, f32[32]{0:T(128)}, f32[32]{0:T(128)}, /*index=5*/f32[32]{0:T(128)}, f32[2048]{0:T(1024)}) all-reduce(f32[1024]{0:T(1024)S(1)} %fusion.168, ...), channel_id=1, replica_groups=mesh['dp'=4,'ctx'=4,'tensor'=2] {'dp','ctx','tensor'}, use_global_device_ids=true, to_apply=%region_34.35 | all-reduce | flops 14688 | bytes 117504 | tf_op jit(solution)/shard_map/psum | solution.py:322
  689.2 26.2 %all-reduce.23.cloned.1.call-done = (bf16[256,1024]{1,0:T(8,128)(2,1)}, bf16[256,1024]{1,0:T(8,128)(2,1)}, bf16[1024,256]{1,0:T(8,128)(2,1)}) async-done(((bf16[256,1024]{1,0:T(8,128)(2,1)}, bf16[256,1024]{1,0:T(8,128)(2,1)}, bf16[1024,256]{1,0:T(8,128)(2,1)}), (bf16[256,1024]{1,0:T(8,128)(2,1)}, bf16[256,1024]{1,0:T(8,128)(2,1)}, bf16[1024,256]{1,0:T(8,128)(2,1)})) %all-reduce.23.cloned.1.call-update) | async-done | bytes 1572880 | tf_op jit(solution)/shard_map/psum | solution.py:291
  (583 shorter events, 205.8 us)
Async XLA Ops:
  7.2 22.2 %copy-start.82 = (f32[4,2304]{1,0:T(4,128)S(1)}, f32[4,2304]{1,0:T(4,128)}, u32[]{:S(2)}) copy-start(f32[4,2304]{1,0:T(4,128)} %param.37) | copy-start | bytes 110596
  7.2 22.2 %slice-start = ((f32[4,2304]{1,0:T(4,128)}), f32[4,256]{1,0:T(4,128)S(1)}, s32[]{:S(2)}) async-start(f32[4,2304]{1,0:T(4,128)} %param.37), calls=%async_computation.16 | async-start | bytes 8192 | tf_op jit(solution)/shard_map/slice | solution.py:152
  7.2 22.3 %copy-start.49 = (bf16[256,256]{1,0:T(8,128)(2,1)S(1)}, bf16[256,256]{1,0:T(8,128)(2,1)}, u32[]{:S(2)}) copy-start(bf16[256,256]{1,0:T(8,128)(2,1)} %param.35) | copy-start | bytes 393220
  7.2 42.0 %all-gather.9.cloned.1.call-start = ((), (), s32[]{:S(2)}) async-start(), calls=%async_computation.4 | async-start | bytes 2621440 | tf_op jit(solution)/shard_map/all_gather | solution.py:124
  7.9 34.8 %copy-start.103 = (f32[32]{0:T(128)S(1)}, f32[32]{0:T(128)}, u32[]{:S(2)}) copy-start(f32[32]{0:T(128)} %param.40) | copy-start | bytes 388
  8.0 35.5 %slice-start.1 = ((f32[2304]{0:T(1024)}), f32[256]{0:T(256)S(1)}, s32[]{:S(2)}) async-start(f32[2304]{0:T(1024)} %param.38), calls=%async_computation.17 | async-start | bytes 2048 | tf_op jit(solution)/shard_map/slice | solution.py:159
  8.0 35.5 %copy-start.98 = (s32[1,256]{1,0:T(1,128)S(1)}, s32[1,256]{1,0:T(1,128)}, u32[]{:S(2)}) copy-start(s32[1,256]{1,0:T(1,128)} %param.30) | copy-start | bytes 3076
  8.0 36.1 %copy-start.8 = (bf16[1,256,1024]{2,1,0:T(8,128)(2,1)S(1)}, bf16[1,256,1024]{2,1,0:T(8,128)(2,1)}, u32[]{:S(2)}) copy-start(bf16[1,256,1024]{2,1,0:T(8,128)(2,1)} %param.29) | copy-start | bytes 1572868
  8.0 36.1 %copy-start.56 = (f32[1024]{0:T(1024)S(1)}, f32[1024]{0:T(1024)}, u32[]{:S(2)}) copy-start(f32[1024]{0:T(1024)} %param.32) | copy-start | bytes 12292
  8.0 210.5 %all-gather.15.cloned.1.call-start = ((), (), s32[]{:S(2)}) async-start(), calls=%async_computation.12 | async-start | bytes 1310720 | tf_op jit(solution)/shard_map/all_gather | solution.py:21
  8.8 36.3 %copy-start.96 = (s32[256]{0:T(256)}, s32[256]{0:T(256)S(1)}, u32[]{:S(2)}) copy-start(s32[256]{0:T(256)S(1)} %get-tuple-element.2175) | copy-start | bytes 3076
  8.9 35.6 %collective-permute-start = (bf16[3]{0:T(256)(128)(2,1)S(1)}, bf16[3]{0:T(256)(128)(2,1)S(1)}, u32[]{:S(2)}, u32[]{:S(2)}) collective-permute-start(bf16[3]{0:T(256)(128)(2,1)S(1)} %slice.175), channel_id=1, source_target_pairs={{0,2},{2,4},{4,6},{1,3},{3,5},{5,7},{8,10},{10,12},{12,14},{9,11},... | collective-permute-start | bytes 26 | tf_op jit(solution)/shard_map/ppermute | solution.py:15
  24.8 19.6 %copy-start.99 = (f32[16]{0:T(128)}, f32[16]{0:T(128)S(1)}, u32[]{:S(2)}) copy-start(f32[16]{0:T(128)S(1)} %fusion.172) | copy-start | bytes 196
  26.1 16.7 %copy-start.90 = (f32[256]{0:T(256)}, f32[256]{0:T(256)S(1)}, u32[]{:S(2)}) copy-start(f32[256]{0:T(256)S(1)} %fusion.118) | copy-start | bytes 3076
  26.1 23.1 %copy-start.73 = (f32[256]{0:T(256)}, f32[256]{0:T(256)S(1)}, u32[]{:S(2)}) copy-start(f32[256]{0:T(256)S(1)} %fusion.171) | copy-start | bytes 3076
  29.5 27.0 %copy-start.59 = (f32[1280]{0:T(1024)}, f32[1280]{0:T(1024)S(1)}, u32[]{:S(2)}) copy-start(f32[1280]{0:T(1024)S(1)} %get-tuple-element.1988) | copy-start | bytes 15364
  29.5 27.0 %copy-start.61 = (f32[1280]{0:T(1024)}, f32[1280]{0:T(1024)S(1)}, u32[]{:S(2)}) copy-start(f32[1280]{0:T(1024)S(1)} %get-tuple-element.1989) | copy-start | bytes 15364
  29.5 27.0 %copy-start.63 = (f32[1280]{0:T(1024)}, f32[1280]{0:T(1024)S(1)}, u32[]{:S(2)}) copy-start(f32[1280]{0:T(1024)S(1)} %get-tuple-element.1990) | copy-start | bytes 15364
  29.5 27.0 %copy-start.65 = (f32[1280]{0:T(1024)}, f32[1280]{0:T(1024)S(1)}, u32[]{:S(2)}) copy-start(f32[1280]{0:T(1024)S(1)} %get-tuple-element.1991) | copy-start | bytes 15364
  46.3 10.2 %copy-start.88 = (f32[256]{0:T(256)}, f32[256]{0:T(256)S(1)}, u32[]{:S(2)}) copy-start(f32[256]{0:T(256)S(1)} %get-tuple-element.2216) | copy-start | bytes 3076
  51.6 4.8 collective-permute-start.1
  188.5 23.2 %copy-start.6 = (f32[2,16,64,128]{3,2,1,0:T(8,128)}, f32[2,16,64,128]{3,2,1,0:T(8,128)S(1)}, u32[]{:S(2)}) copy-start(f32[2,16,64,128]{3,2,1,0:T(8,128)S(1)} %get-tuple-element.2912) | copy-start | bytes 3145732
  188.6 20.0 %copy-start.92 = (f32[256]{0:T(256)S(1)}, f32[256]{0:T(256)}, u32[]{:S(2)}) copy-start(f32[256]{0:T(256)} %get-tuple-element.2217) | copy-start | bytes 3076
  189.3 65.6 %all-gather.11.cloned.1.call-start = ((), (), s32[]{:S(2)}) async-start(), calls=%async_computation.5 | async-start | bytes 2621440 | tf_op jit(solution)/shard_map/all_gather | solution.py:123
  190.1 101.6 %all-gather.13.cloned.1.call-start = ((), (), s32[]{:S(2)}) async-start(), calls=%async_computation.6 | async-start | bytes 2621440 | tf_op jit(solution)/shard_map/all_gather | solution.py:127
  190.7 144.4 %all-gather.17.cloned.1.call-start = ((), (), s32[]{:S(2)}) async-start(), calls=%async_computation.13 | async-start | bytes 1310720 | tf_op jit(solution)/shard_map/all_gather | solution.py:46
  192.0 26.5 %copy-start.44 = (f32[16,2,128]{2,0,1:T(8,128)}, f32[16,2,128]{2,0,1:T(8,128)S(1)}, u32[]{:S(2)}) copy-start(f32[16,2,128]{2,0,1:T(8,128)S(1)} %reduce-window.14) | copy-start | bytes 49156
  192.2 26.3 %copy-start.94 = (f32[16,2]{0,1:T(2,128)}, f32[16,2]{0,1:T(2,128)S(1)}, u32[]{:S(2)}) copy-start(f32[16,2]{0,1:T(2,128)S(1)} %slice.198) | copy-start | bytes 388
  193.5 113.5 %copy-start.47 = (f32[1024]{0:T(1024)}, f32[1024]{0:T(1024)S(1)}, u32[]{:S(2)}) copy-start(f32[1024]{0:T(1024)S(1)} %dynamic_slice.377) | copy-start | bytes 12292
  208.7 95.3 %copy-start.42 = (f32[256,16]{0,1:T(8,128)}, f32[256,16]{0,1:T(8,128)S(1)}, u32[]{:S(2)}) copy-start(f32[256,16]{0,1:T(8,128)S(1)} %fusion.149) | copy-start | bytes 49156
  226.9 28.0 %copy-start.57 = (f32[1024]{0:T(1024)S(1)}, f32[1024]{0:T(1024)}, u32[]{:S(2)}) copy-start(f32[1024]{0:T(1024)} %param.32) | copy-start | bytes 12292
  226.9 28.0 %copy-start.74 = (f32[256]{0:T(256)S(1)}, f32[256]{0:T(256)}, u32[]{:S(2)}) copy-start(f32[256]{0:T(256)} %copy-done.73) | copy-start | bytes 3076
  229.6 62.1 %copy-start.23 = (bf16[1,256,1024]{2,1,0:T(8,128)(2,1)S(1)}, bf16[1,256,1024]{2,1,0:T(8,128)(2,1)}, u32[]{:S(2)}) copy-start(bf16[1,256,1024]{2,1,0:T(8,128)(2,1)} %param.31) | copy-start | bytes 1572868
  258.6 37.1 %copy-start.13 = (f32[256,1024]{1,0:T(8,128)}, f32[256,1024]{1,0:T(8,128)S(1)}, u32[]{:S(2)}) copy-start(f32[256,1024]{1,0:T(8,128)S(1)} %get-tuple-element.2171) | copy-start | bytes 3145732
  261.0 46.0 %copy-start.70 = (f32[256]{0:T(256)}, f32[256]{0:T(256)S(1)}, u32[]{:S(2)}) copy-start(f32[256]{0:T(256)S(1)} %add_rsqrt_fusion) | copy-start | bytes 3076
  306.9 134.4 %reduce-scatter.11.cloned.1.call-start = ((), (), s32[]{:S(2)}) async-start(), calls=%async_computation.11 | async-start | bytes 2621440 | tf_op jit(solution)/shard_map/reduce_scatter | solution.py:286
  310.5 130.8 %reduce-scatter.5.cloned.1.call-start = ((), (), s32[]{:S(2)}) async-start(), calls=%async_computation.7 | async-start | bytes 2621440 | tf_op jit(solution)/shard_map/reduce_scatter | solution.py:277
  317.9 139.9 %reduce-scatter.7.cloned.1.call-start = ((), (), s32[]{:S(2)}) async-start(), calls=%async_computation.8 | async-start | bytes 2621440 | tf_op jit(solution)/shard_map/reduce_scatter | solution.py:280
  416.1 5.7 collective-permute-start.2
  424.3 59.7 %reduce-scatter.9.cloned.1.call-start = ((), (), s32[]{:S(2)}) async-start(), calls=%async_computation.10 | async-start | bytes 40960 | tf_op jit(solution)/shard_map/reduce_scatter | solution.py:283
  434.4 185.8 %all-reduce.21.cloned.1.call-start = ((), (), s32[]{:S(2)}) async-start(), calls=%async_computation.9 | async-start | bytes 2097152 | tf_op jit(solution)/shard_map/psum | solution.py:322
  435.9 205.8 %all-reduce.25.cloned.1.call-start = ((), (), s32[]{:S(2)}) async-start(), calls=%async_computation.15 | async-start | bytes 2097152 | tf_op jit(solution)/shard_map/psum | solution.py:232
  440.3 18.1 %copy-start.79 = (f32[16]{0:T(128)S(1)}, f32[16]{0:T(128)}, u32[]{:S(2)}) copy-start(f32[16]{0:T(128)} %get-tuple-element.3090) | copy-start | bytes 196
  440.3 275.1 %all-reduce.23.cloned.1.call-start = ((), (), s32[]{:S(2)}) async-start(), calls=%async_computation.14 | async-start | bytes 3145728 | tf_op jit(solution)/shard_map/psum | solution.py:291
  457.8 229.8 %copy-start.91 = (f32[256]{0:T(256)S(1)}, f32[256]{0:T(256)}, u32[]{:S(2)}) copy-start(f32[256]{0:T(256)} %copy-done.90) | copy-start | bytes 3076
  457.8 229.8 %copy-start.24 = (bf16[1,256,1024]{2,1,0:T(8,128)(2,1)S(1)}, bf16[1,256,1024]{2,1,0:T(8,128)(2,1)}, u32[]{:S(2)}) copy-start(bf16[1,256,1024]{2,1,0:T(8,128)(2,1)} %param.31) | copy-start | bytes 1572868
  641.7 46.0 %copy-start.29 = (bf16[256,1024]{1,0:T(8,128)(2,1)S(1)}, bf16[256,1024]{1,0:T(8,128)(2,1)}, u32[]{:S(2)}) copy-start(bf16[256,1024]{1,0:T(8,128)(2,1)} %get-tuple-element.2155) | copy-start | bytes 1572868
  641.7 46.0 %copy-start.39 = (bf16[256,1024]{1,0:T(8,128)(2,1)S(1)}, bf16[256,1024]{1,0:T(8,128)(2,1)}, u32[]{:S(2)}) copy-start(bf16[256,1024]{1,0:T(8,128)(2,1)} %get-tuple-element.2154) | copy-start | bytes 1572868
  (100 other events, 273.4 us)
Sparse Core Ops, SparseCore 0:
  9.9 39.2 all-gather.8
  189.5 28.9 all-gather.14
  220.3 34.5 all-gather.10
  256.6 35.0 all-gather.12
  307.0 27.9 all-gather.16
  337.9 34.5 reduce-scatter.10
  375.5 35.2 reduce-scatter.4
  424.4 33.3 reduce-scatter.6
  461.1 22.8 reduce-scatter.8
  489.6 130.5 all-reduce.20
  623.2 18.4 all-reduce.24
  644.1 71.3 all-reduce.22
where the time goes:
time: 741 us; the launch traced here: 727 us
  waiting for transfers between devices  300 us (40%)
  local copies, waits for them, and re-layouts  132 us (18%)
  blocking collectives  96.4 us (13%)
  other arithmetic  85.2 us (11%)
  matrix products  82.3 us (11%)
  between operations  17.8 us (2%)
  starting transfers between devices  10.1 us (1%)
    psum x1, waiting for transfers between devices, body(): lax.psum((gain_term, kernel_term, offset_term, bias_term, decay_term, ski...  124 us
    dynamic_update_slice x32, local copies, waits for them, and re-layouts, block(): lax.scan(partial(group_step, rates=rates), jnp.zeros((local_heads, head_s...  60.8 us
    psum x1, blocking collectives, body(): lax.psum((gain_term, kernel_term, offset_term, bias_term, decay_term, ski...  44.3 us
    all_gather x1, waiting for transfers between devices, body(): lax.all_gather(out_weight, 'dp', axis=1, tiled=True)  30.6 us
    psum x1, waiting for transfers between devices, body(): lax.psum(pieces[0].astype(jnp.bfloat16), 'ctx').astype(jnp.float32)  26.2 us
    reduce_scatter x1, waiting for transfers between devices, body(): lax.psum_scatter(grad_step_w.astype(jnp.bfloat16), 'dp', scatter_dimensio...  25.4 us
    all_gather x1, waiting for transfers between devices, body(): lax.all_gather(gate_weight, 'dp', axis=0, tiled=True)  25.3 us
    psum x1, waiting for transfers between devices, body(): lax.psum(branch_out.astype(jnp.bfloat16), 'tensor').astype(jnp.float32)  19.8 us
  transfers between devices with their start and end apart: 15, of which 12 were waited for; matrix products, arithmetic and copies ran while one was open for 20% of the time, Pallas kernels for 0%

commit v1 on v0

--- a/solution.py
+++ b/solution.py
@@ -319,7 +319,7 @@
     mgain_term = lax.dynamic_update_slice(
         jnp.zeros((inner_width,), jnp.float32), grad_mgain, (shard * local_width,)
     )
-    totals = lax.psum(
+    half = lax.psum(
         (
             gain_term,
             kernel_term,
@@ -330,8 +330,9 @@
             mgain_term,
             grad_state_w,
         ),
-        ("dp", "ctx", "tensor"),
-    )
+        ("ctx", "tensor"),
+    )
+    totals = lax.psum(half, "dp")
     rows = state_weight.shape[0]
     state_rows = lax.dynamic_slice_in_dim(totals[7], lax.axis_index("dp") * rows, rows, 0)
     return (

time: 741 us -> 795 us (1.073)
  waiting for transfers between devices: 300 us -> 352 us
    psum x1, waiting for transfers between devices: 124 us -> 33.6 us  [body(): lax.psum((gain_term, kernel_term, offset_term, bias_term, decay_term, ski...]
    psum x1, waiting for transfers between devices: 26.2 us -> 70 us  [body(): lax.psum(pieces[0].astype(jnp.bfloat16), 'ctx').astype(jnp.float32)]
    reduce_scatter x1, waiting for transfers between devices: 0.02 us -> 38.2 us  [body(): lax.psum_scatter(grad_gate_w.astype(jnp.bfloat16), 'dp', scatter_dimensio...]
    reduce_scatter x1, waiting for transfers between devices: 0.02 us -> 36.3 us  [body(): lax.psum_scatter(grad_out.astype(jnp.bfloat16), 'dp', scatter_dimension=1...]
    reduce_scatter x1, waiting for transfers between devices: 16.5 us -> 38.2 us  [body(): lax.psum_scatter(grad_value_w.astype(jnp.bfloat16), 'dp', scatter_dimensi...]
    psum x0 -> x1, blocking collectives: none -> 18.4 us  [body(): totals = lax.psum(half, 'dp')]
    psum x1, blocking collectives: 44.3 us -> 29.8 us  [body(): lax.psum((gain_term, kernel_term, offset_term, bias_term, decay_term, ski...]
    psum x1, waiting for transfers between devices: 19.8 us -> 9.93 us  [body(): lax.psum(branch_out.astype(jnp.bfloat16), 'tensor').astype(jnp.float32)]
  transfers between devices with their start and end apart: 15 -> 16, of which waited for: 12 -> 15; matrix products, arithmetic and copies ran while one was open for 20% -> 8% of each run, Pallas kernels for 0% -> 0%
where the time goes in v1:
time: 795 us; the launch traced here: 781 us
  waiting for transfers between devices  352 us (44%)
  local copies, waits for them, and re-layouts  129 us (16%)
  blocking collectives  100 us (13%)
  other arithmetic  86.4 us (11%)
  matrix products  81.9 us (10%)
  between operations  17.7 us (2%)
  starting transfers between devices  10.4 us (1%)
    psum x1, waiting for transfers between devices, body(): lax.psum(pieces[0].astype(jnp.bfloat16), 'ctx').astype(jnp.float32)  70 us
    dynamic_update_slice x32, local copies, waits for them, and re-layouts, block(): lax.scan(partial(group_step, rates=rates), jnp.zeros((local_heads, head_s...  61.1 us
    reduce_scatter x1, waiting for transfers between devices, body(): lax.psum_scatter(grad_gate_w.astype(jnp.bfloat16), 'dp', scatter_dimensio...  38.2 us
    reduce_scatter x1, waiting for transfers between devices, body(): lax.psum_scatter(grad_value_w.astype(jnp.bfloat16), 'dp', scatter_dimensi...  38.2 us
    reduce_scatter x1, waiting for transfers between devices, body(): lax.psum_scatter(grad_out.astype(jnp.bfloat16), 'dp', scatter_dimension=1...  36.3 us
    psum x1, waiting for transfers between devices, body(): lax.psum((gain_term, kernel_term, offset_term, bias_term, decay_term, ski...  33.6 us
    all_gather x1, waiting for transfers between devices, body(): lax.all_gather(out_weight, 'dp', axis=1, tiled=True)  30.6 us
    psum x1, blocking collectives, body(): lax.psum((gain_term, kernel_term, offset_term, bias_term, decay_term, ski...  29.8 us
  transfers between devices with their start and end apart: 16, of which 15 were waited for; matrix products, arithmetic and copies ran while one was open for 8% of the time, Pallas kernels for 0%

profile of v1, /device:TPU:0, one launch (start us, length us, event | category | flops | bytes accessed | tf_op | source)
XLA Modules:
  0.0 781.0 jit_solution(5379906702736103072)
XLA Ops:
  8.9 4.9 collective-permute-start
  15.5 8.6 %all_gather.33 = bf16[1024,16]{0,1:T(8,128)(2,1)S(1)} all-gather(bf16[256,16]{0,1:T(8,128)(2,1)} %param.36), channel_id=1, replica_groups=mesh['dp'=4,'ctx'=4,'tensor'=2] {'dp'}, dimensions={0}, use_global_device_ids=true | all-gather | bytes 40960 | tf_op jit(solution)/shard_map/all_gather | solution.py:126
  26.1 2.6 compare_select_fusion.3
  29.5 13.3 %all_gather.35 = bf16[1024,256]{1,0:T(8,128)(2,1)S(1)} all-gather(bf16[256,256]{1,0:T(8,128)(2,1)S(1)} %copy-done.52), channel_id=1, replica_groups=mesh['dp'=4,'ctx'=4,'tensor'=2] {'dp'}, dimensions={0}, use_global_device_ids=true | all-gather | bytes 655360 | tf_op jit(solution)/shard_map/all_gather | solution.py:125
  46.4 2.8 all-gather.9.cloned.1.call-done
  51.6 3.4 collective-permute-start.1
  67.7 121.3 %while.117 = (s32[]{:T(128)}, f32[16,64,128]{2,1,0:T(8,128)S(1)}, f32[2,128,16,64]{1,0,3,2:T(2,128)}, pred[2,16,128,128]{3,2,1,0:T(32,128)(4,1)}, f32[2,16,128,1...) while((s32[]{:T(128)}, f32[16,64,128]{2,1,0:T(8,128)S(1)}, ...), condition=%wide.region_3.4_spmd.clone, body=%wide.region_1.3_spmd.clone.sunk | while | flops 633275392 | bytes 14210707 | solution.py:199
  76.5 3.3 multiply_dynamic-update-slice_fusion.3
  85.9 3.0 fusion.255
  88.9 13.1 %dynamic_update_slice.320 = f32[2,128,16,64]{1,0,3,2:T(2,128)} dynamic-update-slice(f32[2,128,16,64]{1,0,3,2:T(2,128)} %get-tuple-element.2797, f32[1,128,16,64]{1,0,3,2:T(1,128)} %bitcast.578, s32[]{:T(128)} %get-tuple-element.2795, s32[]{:T(128)} %constant.380.clone.1..sunk.1, s32[]{:T(128)} %constant.380.clone.1..sunk.1, s32[]{:T(128)} %constant.380.clone.1..sunk.1) | dynamic-update-slice | bytes 1048580 | tf_op jit(solution)/shard_map/jvp()/while/body/jit(dynamic_update_index_in_dim)/dynamic_update_slice | solution.py:199
  137.1 3.3 multiply_dynamic-update-slice_fusion.3
  146.5 3.0 fusion.255
  149.5 13.1 %dynamic_update_slice.320 = f32[2,128,16,64]{1,0,3,2:T(2,128)} dynamic-update-slice(f32[2,128,16,64]{1,0,3,2:T(2,128)} %get-tuple-element.2797, f32[1,128,16,64]{1,0,3,2:T(1,128)} %bitcast.578, s32[]{:T(128)} %get-tuple-element.2795, s32[]{:T(128)} %constant.380.clone.1..sunk.1, s32[]{:T(128)} %constant.380.clone.1..sunk.1, s32[]{:T(128)} %constant.380.clone.1..sunk.1) | dynamic-update-slice | bytes 1048580 | tf_op jit(solution)/shard_map/jvp()/while/body/jit(dynamic_update_index_in_dim)/dynamic_update_slice | solution.py:199
  195.6 13.5 %all-reduce.13 = bf16[64]{0:T(256)(128)(2,1)S(1)} all-reduce(bf16[64]{0:T(256)(128)(2,1)S(1)} %dynamic-update-slice.8), channel_id=2, replica_groups=mesh['dp'=4,'ctx'=4,'tensor'=2] {'ctx'}, use_global_device_ids=true, to_apply=%add.13 | all-reduce | flops 64 | bytes 256
  209.3 3.0 reshape.727
  212.3 6.7 all-gather.15.cloned.1.call-done
  219.0 4.6 while.118
  223.6 3.8 multiply_add_fusion.2
  227.4 2.6 copy.192
  230.0 25.4 %all-gather.11.cloned.1.call-done = bf16[1024,1024]{1,0:T(8,128)(2,1)} async-done(((bf16[256,1024]{1,0:T(8,128)(2,1)}), bf16[1024,1024]{1,0:T(8,128)(2,1)}) %all-gather.11.cloned.1.call-update) | async-done | bytes 2097168 | tf_op jit(solution)/shard_map/all_gather | solution.py:123
  255.4 3.7 multiply_reduce_fusion.9
  259.1 2.4 psum.168
  261.5 30.6 %all-gather.13.cloned.1.call-done = bf16[1024,1024]{1,0:T(8,128)(2,1)} async-done(((bf16[1024,256]{1,0:T(8,128)(2,1)}), bf16[1024,1024]{1,0:T(8,128)(2,1)}) %all-gather.13.cloned.1.call-update) | async-done | bytes 2097168 | tf_op jit(solution)/shard_map/all_gather | solution.py:127
  292.2 4.0 multiply_reduce_fusion.5
  296.2 2.4 psum.170
  298.7 4.2 multiply_reduce_fusion.6
  303.3 2.7 convolution_convert_fusion.5
  311.0 23.2 %all-gather.17.cloned.1.call-done = bf16[64,64,128]{2,1,0:T(8,128)(2,1)} async-done(((bf16[16,64,128]{2,1,0:T(8,128)(2,1)}), bf16[64,64,128]{2,1,0:T(8,128)(2,1)}) %all-gather.17.cloned.1.call-update) | async-done | bytes 1048592 | tf_op jit(solution)/shard_map/all_gather | solution.py:46
  334.2 3.6 while.116
  341.0 62.2 %while.119 = (s32[]{:T(128)}, f32[16]{0:T(128)}, f32[16,64,128]{2,1,0:T(8,128)S(1)}, f32[2,128,16,64]{1,3,2,0:T(8,128)}, f32[2,128,128]{2,1,0:T(8,128)}, /*index...) while((s32[]{:T(128)}, f32[16]{0:T(128)}, ...), condition=%wide.region_26.27_spmd.clone, body=%wide.region_16.26_spmd.clone.sunk | while | flops 1263052800 | bytes 29513872 | solution.py:199
  345.4 4.8 fusion.271
  376.0 4.8 fusion.271
  403.2 3.3 fusion.113
  415.7 3.8 collective-permute-done.2
  432.2 2.5 reduce-window.16
  434.9 2.5 fusion.195
  440.8 2.4 convolution_add_fusion.6
  445.2 33.6 %all-reduce.23.cloned.1.call-done = f32[1024,256]{1,0:T(8,128)} async-done(((f32[1024,256]{1,0:T(8,128)}), f32[1024,256]{1,0:T(8,128)}) %all-reduce.23.cloned.1.call-update) | async-done | bytes 1048592 | tf_op jit(solution)/shard_map/psum | solution.py:322
  479.7 36.3 %reduce-scatter.11.cloned.1.call-done = bf16[1024,256]{1,0:T(8,128)(2,1)} async-done(((bf16[1024,1024]{1,0:T(8,128)(2,1)}), bf16[1024,256]{1,0:T(8,128)(2,1)}) %reduce-scatter.11.cloned.1.call-update) | async-done | bytes 524304 | tf_op jit(solution)/shard_map/reduce_scatter | solution.py:286
  516.0 38.2 %reduce-scatter.5.cloned.1.call-done = bf16[256,1024]{1,0:T(8,128)(2,1)} async-done(((bf16[1024,1024]{1,0:T(8,128)(2,1)}), bf16[256,1024]{1,0:T(8,128)(2,1)}) %reduce-scatter.5.cloned.1.call-update) | async-done | bytes 524304 | tf_op jit(solution)/shard_map/reduce_scatter | solution.py:277
  554.2 38.2 %reduce-scatter.7.cloned.1.call-done = bf16[256,1024]{1,0:T(8,128)(2,1)} async-done(((bf16[1024,1024]{1,0:T(8,128)(2,1)}), bf16[256,1024]{1,0:T(8,128)(2,1)}) %reduce-scatter.7.cloned.1.call-update) | async-done | bytes 524304 | tf_op jit(solution)/shard_map/reduce_scatter | solution.py:280
  593.2 25.3 %reduce-scatter.9.cloned.1.call-done = bf16[256,16]{0,1:T(8,128)(2,1)} async-done(((bf16[1024,16]{0,1:T(8,128)(2,1)}), bf16[256,16]{0,1:T(8,128)(2,1)}) %reduce-scatter.9.cloned.1.call-update) | async-done | bytes 8208 | tf_op jit(solution)/shard_map/reduce_scatter | solution.py:283
  618.5 12.0 %psum.178 = bf16[256,16]{0,1:T(8,128)(2,1)S(1)} all-reduce(bf16[256,16]{0,1:T(8,128)(2,1)} %reduce-scatter.9.cloned.1.call-done), channel_id=1, replica_groups=mesh['dp'=4,'ctx'=4,'tensor'=2] {'ctx'}, use_global_device_ids=true, to_apply=%region_43.44 | all-reduce | flops 4096 | bytes 16384 | tf_op jit(solution)/shard_map/psum | solution.py:293
  631.0 9.9 %all-reduce.29.cloned.1.call-done = (bf16[256,1024]{1,0:T(8,128)(2,1)}, bf16[256,1024]{1,0:T(8,128)(2,1)}) async-done(((bf16[256,1024]{1,0:T(8,128)(2,1)}, bf16[256,1024]{1,0:T(8,128)(2,1)}), (bf16[256,1024]{1,0:T(8,128)(2,1)}, bf16[256,1024]{1,0:T(8,128)(2,1)})) %all-reduce.29.cloned.1.call-update) | async-done | bytes 1048592 | tf_op jit(solution)/shard_map/psum | solution.py:232
  642.6 29.8 %all-reduce.14 = (f32[1024]{0:T(1024)S(1)}, f32[4,2304]{1,0:T(4,128)S(1)}, f32[2304]{0:T(1024)S(1)}, f32[32]{0:T(128)S(1)}, f32[32]{0:T(128)S(1)}, /*index=5*/f32[32]{0:T(128)S(1)}, f32[2048]{0:T(1024)S(1)}) all-reduce(f32[1024]{0:T(1024)S(1)} %fusion.168, ...), channel_id=1, replica_groups=mesh['dp'=4,'ctx'=4,'tensor'=2] {'ctx','tensor'}, use_global_device_ids=true, to_apply=%region_34.35 | all-reduce | flops 14688 | bytes 117504 | tf_op jit(solution)/shard_map/psum | solution.py:322
  672.4 18.4 %all-reduce.15 = (f32[1024]{0:T(1024)}, f32[4,2304]{1,0:T(4,128)}, f32[2304]{0:T(1024)}, f32[32]{0:T(128)}, f32[32]{0:T(128)}, /*index=5*/f32[32]{0:T(128)}, f32[2048]{0:T(1024)}) all-reduce(f32[1024]{0:T(1024)S(1)} %get-tuple-element.2144, ...), channel_id=1, replica_groups=mesh['dp'=4,'ctx'=4,'tensor'=2] {'dp'}, use_global_device_ids=true, to_apply=%region_35.36 | all-reduce | flops 14688 | bytes 117504 | tf_op jit(solution)/shard_map/psum | solution.py:335
  692.4 5.6 all-reduce.25.cloned.1.call-done
  699.7 70.0 %all-reduce.27.cloned.1.call-done = (bf16[256,1024]{1,0:T(8,128)(2,1)}, bf16[256,1024]{1,0:T(8,128)(2,1)}, bf16[1024,256]{1,0:T(8,128)(2,1)}) async-done(((bf16[256,1024]{1,0:T(8,128)(2,1)}, bf16[256,1024]{1,0:T(8,128)(2,1)}, bf16[1024,256]{1,0:T(8,128)(2,1)}), (bf16[256,1024]{1,0:T(8,128)(2,1)}, bf16[256,1024]{1,0:T(8,128)(2,1)}, bf16[1024,256]{1,0:T(8,128)(2,1)})) %all-reduce.27.cloned.1.call-update) | async-done | bytes 1572880 | tf_op jit(solution)/shard_map/psum | solution.py:291
  (593 shorter events, 215.8 us)
Async XLA Ops:
  7.2 22.3 %copy-start.52 = (bf16[256,256]{1,0:T(8,128)(2,1)S(1)}, bf16[256,256]{1,0:T(8,128)(2,1)}, u32[]{:S(2)}) copy-start(bf16[256,256]{1,0:T(8,128)(2,1)} %param.35) | copy-start | bytes 393220
  7.2 42.0 %all-gather.9.cloned.1.call-start = ((), (), s32[]{:S(2)}) async-start(), calls=%async_computation.4 | async-start | bytes 2621440 | tf_op jit(solution)/shard_map/all_gather | solution.py:124
  7.9 34.9 %copy-start.106 = (f32[32]{0:T(128)S(1)}, f32[32]{0:T(128)}, u32[]{:S(2)}) copy-start(f32[32]{0:T(128)} %param.40) | copy-start | bytes 388
  8.0 35.6 %slice-start.1 = ((f32[2304]{0:T(1024)}), f32[256]{0:T(256)S(1)}, s32[]{:S(2)}) async-start(f32[2304]{0:T(1024)} %param.38), calls=%async_computation.18 | async-start | bytes 2048 | tf_op jit(solution)/shard_map/slice | solution.py:159
  8.0 35.6 %copy-start.101 = (s32[1,256]{1,0:T(1,128)S(1)}, s32[1,256]{1,0:T(1,128)}, u32[]{:S(2)}) copy-start(s32[1,256]{1,0:T(1,128)} %param.30) | copy-start | bytes 3076
  8.0 36.1 %copy-start.8 = (bf16[1,256,1024]{2,1,0:T(8,128)(2,1)S(1)}, bf16[1,256,1024]{2,1,0:T(8,128)(2,1)}, u32[]{:S(2)}) copy-start(bf16[1,256,1024]{2,1,0:T(8,128)(2,1)} %param.29) | copy-start | bytes 1572868
  8.0 36.1 %copy-start.59 = (f32[1024]{0:T(1024)S(1)}, f32[1024]{0:T(1024)}, u32[]{:S(2)}) copy-start(f32[1024]{0:T(1024)} %param.32) | copy-start | bytes 12292
  8.0 211.0 %all-gather.15.cloned.1.call-start = ((), (), s32[]{:S(2)}) async-start(), calls=%async_computation.13 | async-start | bytes 1310720 | tf_op jit(solution)/shard_map/all_gather | solution.py:21
  8.8 36.4 %copy-start.99 = (s32[256]{0:T(256)}, s32[256]{0:T(256)S(1)}, u32[]{:S(2)}) copy-start(s32[256]{0:T(256)S(1)} %get-tuple-element.2182) | copy-start | bytes 3076
  8.9 35.6 %collective-permute-start = (bf16[3]{0:T(256)(128)(2,1)S(1)}, bf16[3]{0:T(256)(128)(2,1)S(1)}, u32[]{:S(2)}, u32[]{:S(2)}) collective-permute-start(bf16[3]{0:T(256)(128)(2,1)S(1)} %slice.175), channel_id=1, source_target_pairs={{0,2},{2,4},{4,6},{1,3},{3,5},{5,7},{8,10},{10,12},{12,14},{9,11},... | collective-permute-start | bytes 26 | tf_op jit(solution)/shard_map/ppermute | solution.py:15
  26.1 23.1 %copy-start.76 = (f32[256]{0:T(256)}, f32[256]{0:T(256)S(1)}, u32[]{:S(2)}) copy-start(f32[256]{0:T(256)S(1)} %fusion.171) | copy-start | bytes 3076
  29.5 27.0 %copy-start.62 = (f32[1280]{0:T(1024)}, f32[1280]{0:T(1024)S(1)}, u32[]{:S(2)}) copy-start(f32[1280]{0:T(1024)S(1)} %get-tuple-element.1988) | copy-start | bytes 15364
  29.5 27.0 %copy-start.64 = (f32[1280]{0:T(1024)}, f32[1280]{0:T(1024)S(1)}, u32[]{:S(2)}) copy-start(f32[1280]{0:T(1024)S(1)} %get-tuple-element.1989) | copy-start | bytes 15364
  29.5 27.0 %copy-start.66 = (f32[1280]{0:T(1024)}, f32[1280]{0:T(1024)S(1)}, u32[]{:S(2)}) copy-start(f32[1280]{0:T(1024)S(1)} %get-tuple-element.1990) | copy-start | bytes 15364
  29.5 27.0 %copy-start.68 = (f32[1280]{0:T(1024)}, f32[1280]{0:T(1024)S(1)}, u32[]{:S(2)}) copy-start(f32[1280]{0:T(1024)S(1)} %get-tuple-element.1991) | copy-start | bytes 15364
  51.6 4.8 collective-permute-start.1
  189.0 23.3 %copy-start.6 = (f32[2,16,64,128]{3,2,1,0:T(8,128)}, f32[2,16,64,128]{3,2,1,0:T(8,128)S(1)}, u32[]{:S(2)}) copy-start(f32[2,16,64,128]{3,2,1,0:T(8,128)S(1)} %get-tuple-element.2919) | copy-start | bytes 3145732
  189.9 65.5 %all-gather.11.cloned.1.call-start = ((), (), s32[]{:S(2)}) async-start(), calls=%async_computation.5 | async-start | bytes 2621440 | tf_op jit(solution)/shard_map/all_gather | solution.py:123
  190.6 101.6 %all-gather.13.cloned.1.call-start = ((), (), s32[]{:S(2)}) async-start(), calls=%async_computation.6 | async-start | bytes 2621440 | tf_op jit(solution)/shard_map/all_gather | solution.py:127
  191.2 143.0 %all-gather.17.cloned.1.call-start = ((), (), s32[]{:S(2)}) async-start(), calls=%async_computation.14 | async-start | bytes 1310720 | tf_op jit(solution)/shard_map/all_gather | solution.py:46
  192.5 26.5 %copy-start.47 = (f32[16,2,128]{2,0,1:T(8,128)}, f32[16,2,128]{2,0,1:T(8,128)S(1)}, u32[]{:S(2)}) copy-start(f32[16,2,128]{2,0,1:T(8,128)S(1)} %reduce-window.14) | copy-start | bytes 49156
  192.7 26.3 %copy-start.97 = (f32[16,2]{0,1:T(2,128)}, f32[16,2]{0,1:T(2,128)S(1)}, u32[]{:S(2)}) copy-start(f32[16,2]{0,1:T(2,128)S(1)} %slice.198) | copy-start | bytes 388
  194.0 104.6 %copy-start.50 = (f32[1024]{0:T(1024)}, f32[1024]{0:T(1024)S(1)}, u32[]{:S(2)}) copy-start(f32[1024]{0:T(1024)S(1)} %dynamic_slice.377) | copy-start | bytes 12292
  209.3 94.0 %copy-start.46 = (f32[256,16]{0,1:T(8,128)}, f32[256,16]{0,1:T(8,128)S(1)}, u32[]{:S(2)}) copy-start(f32[256,16]{0,1:T(8,128)S(1)} %fusion.149) | copy-start | bytes 49156
  227.4 28.0 %copy-start.60 = (f32[1024]{0:T(1024)S(1)}, f32[1024]{0:T(1024)}, u32[]{:S(2)}) copy-start(f32[1024]{0:T(1024)} %param.32) | copy-start | bytes 12292
  227.4 28.0 %copy-start.77 = (f32[256]{0:T(256)S(1)}, f32[256]{0:T(256)}, u32[]{:S(2)}) copy-start(f32[256]{0:T(256)} %copy-done.76) | copy-start | bytes 3076
  230.0 62.2 %copy-start.26 = (bf16[1,256,1024]{2,1,0:T(8,128)(2,1)S(1)}, bf16[1,256,1024]{2,1,0:T(8,128)(2,1)}, u32[]{:S(2)}) copy-start(bf16[1,256,1024]{2,1,0:T(8,128)(2,1)} %param.31) | copy-start | bytes 1572868
  259.1 39.6 %copy-start.14 = (f32[256,1024]{1,0:T(8,128)}, f32[256,1024]{1,0:T(8,128)S(1)}, u32[]{:S(2)}) copy-start(f32[256,1024]{1,0:T(8,128)S(1)} %get-tuple-element.2178) | copy-start | bytes 3145732
  261.5 37.1 %copy-start.73 = (f32[256]{0:T(256)}, f32[256]{0:T(256)S(1)}, u32[]{:S(2)}) copy-start(f32[256]{0:T(256)S(1)} %add_rsqrt_fusion) | copy-start | bytes 3076
  306.0 172.7 %all-reduce.23.cloned.1.call-start = ((), (), s32[]{:S(2)}) async-start(), calls=%async_computation.9 | async-start | bytes 2097152 | tf_op jit(solution)/shard_map/psum | solution.py:322
  413.7 5.7 collective-permute-start.2
  421.2 94.8 %reduce-scatter.11.cloned.1.call-start = ((), (), s32[]{:S(2)}) async-start(), calls=%async_computation.12 | async-start | bytes 2621440 | tf_op jit(solution)/shard_map/reduce_scatter | solution.py:286
  423.9 130.3 %reduce-scatter.5.cloned.1.call-start = ((), (), s32[]{:S(2)}) async-start(), calls=%async_computation.7 | async-start | bytes 2621440 | tf_op jit(solution)/shard_map/reduce_scatter | solution.py:277
  427.2 165.2 %reduce-scatter.7.cloned.1.call-start = ((), (), s32[]{:S(2)}) async-start(), calls=%async_computation.8 | async-start | bytes 2621440 | tf_op jit(solution)/shard_map/reduce_scatter | solution.py:280
  429.6 188.9 %reduce-scatter.9.cloned.1.call-start = ((), (), s32[]{:S(2)}) async-start(), calls=%async_computation.11 | async-start | bytes 40960 | tf_op jit(solution)/shard_map/reduce_scatter | solution.py:283
  440.5 200.5 %all-reduce.29.cloned.1.call-start = ((), (), s32[]{:S(2)}) async-start(), calls=%async_computation.16 | async-start | bytes 2097152 | tf_op jit(solution)/shard_map/psum | solution.py:232
  445.1 33.8 %copy-start.83 = (f32[1024]{0:T(1024)S(1)}, f32[1024]{0:T(1024)}, u32[]{:S(2)}) copy-start(f32[1024]{0:T(1024)} %get-tuple-element.2170) | copy-start | bytes 12292
  445.1 34.2 %copy-start.86 = (f32[1024]{0:T(1024)S(1)}, f32[1024]{0:T(1024)}, u32[]{:S(2)}) copy-start(f32[1024]{0:T(1024)} %get-tuple-element.1983) | copy-start | bytes 12292
  445.1 34.5 %copy-start.81 = (f32[1280]{0:T(1024)S(1)}, f32[1280]{0:T(1024)}, u32[]{:S(2)}) copy-start(f32[1280]{0:T(1024)} %get-tuple-element.1979) | copy-start | bytes 15364
  445.1 34.5 %copy-start.80 = (f32[1280]{0:T(1024)S(1)}, f32[1280]{0:T(1024)}, u32[]{:S(2)}) copy-start(f32[1280]{0:T(1024)} %get-tuple-element.1980) | copy-start | bytes 15364
  445.1 34.5 %copy-start.79 = (f32[1280]{0:T(1024)S(1)}, f32[1280]{0:T(1024)}, u32[]{:S(2)}) copy-start(f32[1280]{0:T(1024)} %get-tuple-element.1981) | copy-start | bytes 15364
  445.1 252.9 %all-reduce.25.cloned.1.call-start = ((), (), s32[]{:S(2)}) async-start(), calls=%async_computation.10 | async-start | bytes 2097152 | tf_op jit(solution)/shard_map/psum | solution.py:335
  478.8 114.3 %copy-start.82 = (f32[16]{0:T(128)S(1)}, f32[16]{0:T(128)}, u32[]{:S(2)}) copy-start(f32[16]{0:T(128)} %get-tuple-element.3101) | copy-start | bytes 196
  478.8 290.9 %all-reduce.27.cloned.1.call-start = ((), (), s32[]{:S(2)}) async-start(), calls=%async_computation.15 | async-start | bytes 3145728 | tf_op jit(solution)/shard_map/psum | solution.py:291
  592.4 98.4 %copy-start.94 = (f32[256]{0:T(256)S(1)}, f32[256]{0:T(256)}, u32[]{:S(2)}) copy-start(f32[256]{0:T(256)} %copy-done.93) | copy-start | bytes 3076
  592.4 98.4 %copy-start.28 = (bf16[1,256,1024]{2,1,0:T(8,128)(2,1)S(1)}, bf16[1,256,1024]{2,1,0:T(8,128)(2,1)}, u32[]{:S(2)}) copy-start(bf16[1,256,1024]{2,1,0:T(8,128)(2,1)} %param.31) | copy-start | bytes 1572868
  641.0 49.9 %copy-start.34 = (bf16[256,1024]{1,0:T(8,128)(2,1)S(1)}, bf16[256,1024]{1,0:T(8,128)(2,1)}, u32[]{:S(2)}) copy-start(bf16[256,1024]{1,0:T(8,128)(2,1)} %get-tuple-element.2162) | copy-start | bytes 1572868
  641.0 49.9 %copy-start.43 = (bf16[256,1024]{1,0:T(8,128)(2,1)S(1)}, bf16[256,1024]{1,0:T(8,128)(2,1)}, u32[]{:S(2)}) copy-start(bf16[256,1024]{1,0:T(8,128)(2,1)} %get-tuple-element.2161) | copy-start | bytes 1572868
  (104 other events, 385.1 us)
Sparse Core Ops, SparseCore 0:
  9.9 39.2 all-gather.8
  190.0 28.9 all-gather.14
  220.8 34.5 all-gather.10
  257.1 35.0 all-gather.12
  306.2 27.9 all-gather.16
  421.3 57.4 all-reduce.22
  481.7 34.2 reduce-scatter.10
  519.0 35.1 reduce-scatter.4
  557.2 35.1 reduce-scatter.6
  595.5 22.8 reduce-scatter.8
  621.4 19.5 all-reduce.28
  643.9 54.0 all-reduce.24
  700.6 69.0 all-reduce.26
